TPU v7x, 32 devices: a whole 2x2x4 slice. The times are simulated.
32 devices in a mesh: rep: 8 (over y, x, core), fsdp: 4 (over z).
Axes of the slice: x: 2, y: 2, z: 4, core: 2. Of those that a mesh axis runs over, the one named last changes fastest.
Arguments:
- tokens: bfloat16 [8, 2048, 1088], P('rep', 'fsdp'), may hold values from -6 to 6
- w_qkv: bfloat16 [1088, 3264], P('fsdp'), may hold values from -0.1875 to 0.1875
- qv_bias: bfloat16 [2176], P('fsdp'), may hold values from -0.29882812 to 0.29882812
- w_out: bfloat16 [1088, 1088], P('fsdp'), may hold values from -1.5 to 1.5
- out_bias: bfloat16 [1088], P('fsdp'), may hold values from -1.796875 to 1.796875
- w_up: bfloat16 [1088, 4352], P('fsdp'), may hold values from -0.1875 to 0.1875
- up_bias: bfloat16 [4352], P('fsdp'), may hold values from -3 to 3
- w_down: bfloat16 [4352, 1088], P('fsdp'), may hold values from -0.09375 to 0.09375
- down_bias: bfloat16 [1088], P('fsdp'), may hold values from -1.796875 to 1.796875
- ln1_gain: bfloat16 [1088], P('fsdp'), may hold values from 0.099609375 to 1.8984375
- ln1_bias: bfloat16 [1088], P('fsdp'), may hold values from -3 to 3
- ln2_gain: bfloat16 [1088], P('fsdp'), may hold values from 0.099609375 to 1.8984375
- ln2_bias: bfloat16 [1088], P('fsdp'), may hold values from -3 to 3
- cotangent: bfloat16 [8, 2048, 1088], P('rep', 'fsdp'), may hold values from -6 to 6
Outputs:
- layer_out: float32 [8, 2048, 1088], P('rep', 'fsdp')
- grad_tokens: float32 [8, 2048, 1088], P('rep', 'fsdp')
- grad_w_qkv: float32 [1088, 3264], P('fsdp')
- grad_qv_bias: float32 [2176], P('fsdp')
- grad_w_out: float32 [1088, 1088], P('fsdp')
- grad_out_bias: float32 [1088], P('fsdp')
- grad_w_up: float32 [1088, 4352], P('fsdp')
- grad_up_bias: float32 [4352], P('fsdp')
- grad_w_down: float32 [4352, 1088], P('fsdp')
- grad_down_bias: float32 [1088], P('fsdp')
- grad_ln1_gain: float32 [1088], P('fsdp')
- grad_ln1_bias: float32 [1088], P('fsdp')
- grad_ln2_gain: float32 [1088], P('fsdp')
- grad_ln2_bias: float32 [1088], P('fsdp')
All inputs are finite; a program needn't handle non-finite values.
Results may differ from a plain program's by a relative error of at most 0.012.
Values may be sent and summed in bfloat16 or wider, within the bound.
No kernel may reach another device: no remote copies, remote signals or barrier semaphores. Data moves between devices by JAX's collectives and lax.ppermute only.
A program may use at most 256 MiB of HBM per device.

v0:
```python
import jax
import jax.numpy as jnp
from jax import lax
from jax.sharding import PartitionSpec as P

HD = 64
EPSILON = 1e-05


def normalize(vector):
    centre = vector - jnp.mean(vector, axis=-1, keepdims=True)
    inverse = lax.rsqrt(jnp.mean(centre * centre, axis=-1, keepdims=True) + EPSILON)
    return centre * inverse


def gelu_exact(vector):
    return jax.nn.gelu(vector, approximate=False)


def local(
    tokens,
    w_qkv,
    qv_bias,
    w_out,
    out_bias,
    w_up,
    up_bias,
    w_down,
    down_bias,
    ln1_gain,
    ln1_bias,
    ln2_gain,
    ln2_bias,
    cotangent,
):
    seq_count, local_len, features = tokens.shape
    rows = w_qkv.shape[0]
    reps = lax.axis_size("rep")
    rep_at = lax.axis_index("rep")
    everyone = ("fsdp", "rep")

    def own_piece(matrix):
        part = matrix.shape[0] // reps
        return lax.dynamic_slice_in_dim(matrix, rep_at * part, part, 0)

    def to_units(matrix):
        blocks = matrix.shape[1] // features
        return matrix.reshape(rows, blocks, features).transpose(1, 0, 2)

    def gather_all(matrix):
        return lax.all_gather(own_piece(matrix), everyone, axis=0, tiled=True)

    def from_units(units):
        blocks = units.shape[1]
        return units.transpose(0, 2, 1, 3).reshape(features, blocks * features)

    pack_one = jnp.concatenate([to_units(w_qkv), to_units(w_out)], 0)
    units_one = gather_all(pack_one.reshape(-1, features)).reshape(-1, 4, rows, features)
    units_up = gather_all(to_units(w_up).reshape(-1, features)).reshape(-1, 4, rows, features)
    down_full = gather_all(w_down)
    qkv_full = from_units(units_one[:, :3])
    out_full = from_units(units_one[:, 3:])
    up_full = from_units(units_up)
    vectors = (qv_bias, out_bias, up_bias, down_bias, ln1_gain, ln1_bias, ln2_gain, ln2_bias)
    small = lax.all_gather(jnp.concatenate(vectors), "fsdp", axis=0)
    pieces = []
    start = 0
    for vector in vectors:
        pieces.append(small[:, start : start + vector.shape[0]].reshape(-1))
        start += vector.shape[0]
    qv_full, outb_full, upb_full, downb_full, gain_one, shift_one, gain_two, shift_two = pieces
    row_count = seq_count * local_len
    total_len = local_len * lax.axis_size("fsdp")
    offset = lax.axis_index("fsdp") * local_len
    head_count = features // HD
    scale = HD ** (-0.5)
    inputs = tokens.reshape(row_count, features).astype(jnp.float32)
    normal_one, pull_one = jax.vjp(normalize, inputs)
    first = (normal_one * gain_one.astype(jnp.float32) + shift_one.astype(jnp.float32)).astype(
        jnp.bfloat16
    )
    qv_wide = qv_full.astype(jnp.float32)
    zero_keys = jnp.zeros((features,), jnp.float32)
    full_bias = jnp.concatenate([qv_wide[:features], zero_keys, qv_wide[features:]])
    mixed = (jnp.dot(first, qkv_full, preferred_element_type=jnp.float32) + full_bias).astype(
        jnp.bfloat16
    )
    queries = mixed[:, :features].reshape(seq_count, local_len, features)
    keys = mixed[:, features : 2 * features].reshape(seq_count, local_len, features)
    values = mixed[:, 2 * features :].reshape(seq_count, local_len, features)
    keys_all, values_all = (
        lax.all_gather(keys, "fsdp", axis=1, tiled=True),
        lax.all_gather(values, "fsdp", axis=1, tiled=True),
    )
    query_pos = offset + jnp.arange(local_len, dtype=jnp.int32)
    key_pos = jnp.arange(total_len, dtype=jnp.int32)
    allowed = key_pos[None, :] <= query_pos[:, None]

    def head_parts(head_index, source):
        column = head_index * HD
        return lax.dynamic_slice_in_dim(source, column, HD, 2)

    def head_scores(query_part, key_part):
        scores = (
            jnp.einsum("sqd,skd->sqk", query_part, key_part, preferred_element_type=jnp.float32)
            * scale
        )
        return jnp.where(allowed[None], scores, -1e30)

    def head_forward(head_index):
        query_part = head_parts(head_index, queries)
        key_part = head_parts(head_index, keys_all)
        value_part = head_parts(head_index, values_all)
        scores = head_scores(query_part, key_part)
        row_peak = jnp.max(scores, axis=-1, keepdims=True)
        weights = jnp.exp(scores - row_peak)
        row_total = jnp.sum(weights, axis=-1, keepdims=True)
        probabilities = (weights / row_total).astype(jnp.bfloat16)
        head_out = jnp.einsum(
            "sqk,skd->sqd", probabilities, value_part, preferred_element_type=jnp.float32
        )
        return (head_out, (row_peak + jnp.log(row_total))[..., 0])

    head_indices = jnp.arange(head_count, dtype=jnp.int32)
    per_head, logsum = lax.map(head_forward, head_indices)
    attended = per_head.transpose(1, 2, 0, 3).reshape(row_count, features).astype(jnp.bfloat16)
    branch = jnp.dot(attended, out_full, preferred_element_type=jnp.float32) + outb_full.astype(
        jnp.float32
    )
    hidden = inputs + branch
    normal_two, pull_two = jax.vjp(normalize, hidden)
    second = (normal_two * gain_two.astype(jnp.float32) + shift_two.astype(jnp.float32)).astype(
        jnp.bfloat16
    )
    upward = jnp.dot(second, up_full, preferred_element_type=jnp.float32) + upb_full.astype(
        jnp.float32
    )
    activated, pull_gelu = jax.vjp(gelu_exact, upward)
    act_low = activated.astype(jnp.bfloat16)
    result = hidden + (
        jnp.dot(act_low, down_full, preferred_element_type=jnp.float32)
        + downb_full.astype(jnp.float32)
    )
    qkv_back, out_back, up_back, down_back, gain_one_back, gain_two_back = (
        qkv_full,
        out_full,
        up_full,
        down_full,
        gain_one,
        gain_two,
    )
    upstream = cotangent.reshape(row_count, features).astype(jnp.float32)
    down_grad = cotangent.reshape(row_count, features)
    grad_down_w = jnp.einsum("rf,rd->fd", act_low, down_grad, preferred_element_type=jnp.float32)
    grad_down_b = jnp.sum(upstream, axis=0)
    grad_act = jnp.einsum("rd,fd->rf", down_grad, down_back, preferred_element_type=jnp.float32)
    (grad_upward,) = pull_gelu(grad_act)
    up_low = grad_upward.astype(jnp.bfloat16)
    grad_up_w = jnp.einsum("rd,rf->df", second, up_low, preferred_element_type=jnp.float32)
    grad_up_b = jnp.sum(up_low.astype(jnp.float32), axis=0)
    grad_second = jnp.einsum("rf,df->rd", up_low, up_back, preferred_element_type=jnp.float32)
    grad_gain_two = jnp.sum(grad_second * normal_two, axis=0)
    grad_shift_two = jnp.sum(grad_second, axis=0)
    (grad_norm_two,) = pull_two(grad_second * gain_two_back.astype(jnp.float32))
    grad_hidden = upstream + grad_norm_two
    branch_grad = grad_hidden.astype(jnp.bfloat16)
    grad_out_w = jnp.einsum("rc,rd->cd", attended, branch_grad, preferred_element_type=jnp.float32)
    grad_out_b = jnp.sum(branch_grad.astype(jnp.float32), axis=0)
    grad_att = jnp.einsum("rd,cd->rc", branch_grad, out_back, preferred_element_type=jnp.float32)
    grad_att = grad_att.astype(jnp.bfloat16).reshape(seq_count, local_len, features)

    def head_backward(head_pair):
        head_index, head_logsum = head_pair
        query_part = head_parts(head_index, queries)
        key_part = head_parts(head_index, keys_all)
        value_part = head_parts(head_index, values_all)
        grad_part = head_parts(head_index, grad_att)
        scores = head_scores(query_part, key_part)
        probabilities = jnp.exp(scores - head_logsum[..., None])
        grad_probs = jnp.einsum(
            "sqd,skd->sqk", grad_part, value_part, preferred_element_type=jnp.float32
        )
        inner_sum = jnp.sum(probabilities * grad_probs, axis=-1, keepdims=True)
        grad_scores = (probabilities * (grad_probs - inner_sum)).astype(jnp.bfloat16)
        grad_query = (
            jnp.einsum("sqk,skd->sqd", grad_scores, key_part, preferred_element_type=jnp.float32)
            * scale
        )
        grad_key = (
            jnp.einsum("sqk,sqd->skd", grad_scores, query_part, preferred_element_type=jnp.float32)
            * scale
        )
        grad_value = jnp.einsum(
            "sqk,sqd->skd",
            probabilities.astype(jnp.bfloat16),
            grad_part,
            preferred_element_type=jnp.float32,
        )
        return (grad_query, grad_key, grad_value)

    query_grads, key_grads, value_grads = lax.map(head_backward, (head_indices, logsum))
    query_grads = query_grads.transpose(1, 2, 0, 3).reshape(seq_count, local_len, features)
    key_grads = key_grads.transpose(1, 2, 0, 3).reshape(seq_count, total_len, features)
    value_grads = value_grads.transpose(1, 2, 0, 3).reshape(seq_count, total_len, features)
    own_keys, own_values = (
        lax.psum_scatter(key_grads.astype(jnp.bfloat16), "fsdp", scatter_dimension=1, tiled=True),
        lax.psum_scatter(value_grads.astype(jnp.bfloat16), "fsdp", scatter_dimension=1, tiled=True),
    )
    mixed_grad = jnp.concatenate([query_grads.astype(jnp.bfloat16), own_keys, own_values], axis=-1)
    mixed_grad = mixed_grad.reshape(row_count, 3 * features)
    grad_qkv_w = jnp.einsum("rd,re->de", first, mixed_grad, preferred_element_type=jnp.float32)
    column_sums = jnp.sum(mixed_grad.astype(jnp.float32), axis=0)
    grad_qv_b = jnp.concatenate([column_sums[:features], column_sums[2 * features :]])
    grad_first = jnp.einsum("re,de->rd", mixed_grad, qkv_back, preferred_element_type=jnp.float32)
    grad_gain_one = jnp.sum(grad_first * normal_one, axis=0)
    grad_shift_one = jnp.sum(grad_first, axis=0)
    (grad_norm_one,) = pull_one(grad_first * gain_one_back.astype(jnp.float32))
    grad_inputs = grad_hidden + grad_norm_one
    fsdp = lax.axis_size("fsdp")

    def grad_units(matrix):
        blocks = matrix.shape[1] // features
        return (
            matrix.astype(jnp.bfloat16).reshape(fsdp, rows, blocks, features).transpose(0, 2, 1, 3)
        )

    def reduce_all(matrix):
        part = lax.psum_scatter(matrix, everyone, scatter_dimension=0, tiled=True)
        return lax.all_gather(part, "rep", axis=0, tiled=True)

    def own_matrix(units):
        blocks = units.shape[0] // rows
        wide = units.reshape(blocks, rows, features).transpose(1, 0, 2)
        return wide.reshape(rows, blocks * features).astype(jnp.float32)

    down_own = reduce_all(grad_down_w.astype(jnp.bfloat16)).astype(jnp.float32)
    up_own = own_matrix(reduce_all(grad_units(grad_up_w).reshape(-1, features)))
    packed = jnp.concatenate([grad_units(grad_qkv_w), grad_units(grad_out_w)], 1)
    one_own = reduce_all(packed.reshape(-1, features))
    qkv_own = own_matrix(one_own[: 3 * rows])
    out_own = own_matrix(one_own[3 * rows :])
    small_grads = (
        grad_qv_b,
        grad_out_b,
        grad_up_b,
        grad_down_b,
        grad_gain_one,
        grad_shift_one,
        grad_gain_two,
        grad_shift_two,
    )
    stacked = jnp.concatenate([g.reshape(fsdp, -1) for g in small_grads], 1)
    stacked = lax.psum(stacked, ("rep", "fsdp"))
    mine = lax.dynamic_index_in_dim(stacked, lax.axis_index("fsdp"), 0, keepdims=False)
    small_own = []
    start = 0
    for g in small_grads:
        width = g.shape[0] // fsdp
        small_own.append(mine[start : start + width])
        start += width
    return (
        result.reshape(seq_count, local_len, features),
        grad_inputs.reshape(seq_count, local_len, features),
        qkv_own,
        small_own[0],
        out_own,
        small_own[1],
        up_own,
        small_own[2],
        down_own,
        small_own[3],
        small_own[4],
        small_own[5],
        small_own[6],
        small_own[7],
    )


def solution(mesh):
    return jax.shard_map(
        local,
        mesh=mesh,
        in_specs=(
            P("rep", "fsdp", None),
            P("fsdp", None),
            P("fsdp"),
            P("fsdp", None),
            P("fsdp"),
            P("fsdp", None),
            P("fsdp"),
            P("fsdp", None),
            P("fsdp"),
            P("fsdp"),
            P("fsdp"),
            P("fsdp"),
            P("fsdp"),
            P("rep", "fsdp", None),
        ),
        out_specs=(
            P("rep", "fsdp", None),
            P("rep", "fsdp", None),
            P("fsdp", None),
            P("fsdp"),
            P("fsdp", None),
            P("fsdp"),
            P("fsdp", None),
            P("fsdp"),
            P("fsdp", None),
            P("fsdp"),
            P("fsdp"),
            P("fsdp"),
            P("fsdp"),
            P("fsdp"),
        ),
        check_vma=False,
    )
```

profile of v0, /device:TPU:0, one launch (start us, length us, event | category | flops | bytes accessed | tf_op | source)
XLA Modules:
  0.0 1485.0 jit_solution(5618912969653301980)
XLA Ops:
  7.3 5.9 reshape.469
  14.2 4.4 pad_maximum_fusion.1
  22.1 6.3 reshape.476
  33.1 21.1 %all-reduce = bf16[13056]{0:T(1024)(128)(2,1)S(1)} all-reduce(bf16[13056]{0:T(1024)(128)(2,1)S(1)} %dynamic-update-slice), channel_id=2, replica_groups=mesh['rep'=8,'fsdp'=4] {'fsdp'}, use_global_device_ids=true, to_apply=%add | all-reduce | flops 13056 | bytes 52224
  58.5 50.7 %all-gather.12.cloned.1.call-done = bf16[4352,1088]{1,0:T(8,128)(2,1)} async-done(((bf16[136,1088]{1,0:T(8,128)(2,1)}), bf16[4352,1088]{1,0:T(8,128)(2,1)}) %all-gather.12.cloned.1.call-update) | async-done | bytes 9469968 | tf_op jit(solution)/shard_map/all_gather | solution.py:51
  109.2 3.7 slice.164
  112.9 10.9 copy.91
  123.8 19.2 %reshape.472 = bf16[1088,3264]{1,0:T(8,128)(2,1)} reshape(bf16[4,272,3,1088]{3,2,1,0:T(4,128)(2,1)} %bitcast.241) | data formatting | bytes 14204928 | tf_op jit(solution)/shard_map/reshape | solution.py:55
  143.0 8.3 add_convert_fusion
  155.3 3.4 slice.171
  159.4 35.9 %all-gather.14.cloned.1.call-done = bf16[4352,1088]{1,0:T(8,128)(2,1)} async-done(((bf16[136,1088]{1,0:T(8,128)(2,1)}), bf16[4352,1088]{1,0:T(8,128)(2,1)}) %all-gather.14.cloned.1.call-update) | async-done | bytes 9469968 | tf_op jit(solution)/shard_map/all_gather | solution.py:51
  195.3 9.7 copy.92
  205.0 16.7 %reshape.479 = bf16[1088,4352]{1,0:T(8,128)(2,1)} reshape(bf16[4,272,4,1088]{3,2,1,0:T(4,128)(2,1)} %bitcast.240) | data formatting | bytes 18939904 | tf_op jit(solution)/shard_map/reshape | solution.py:55
  221.6 59.5 %all-gather.24.cloned.1.call-done = bf16[2048,1088]{0,1:T(8,128)(2,1)} async-done(((bf16[512,1088]{0,1:T(8,128)(2,1)}), bf16[2048,1088]{0,1:T(8,128)(2,1)}) %all-gather.24.cloned.1.call-update) | async-done | bytes 4456464 | tf_op jit(solution)/shard_map/all_gather | solution.py:92
  281.1 6.4 copy.73
  287.5 79.1 %all-gather.26.cloned.1.call-done = bf16[2048,1088]{0,1:T(8,128)(2,1)} async-done(((bf16[512,1088]{0,1:T(8,128)(2,1)}), bf16[2048,1088]{0,1:T(8,128)(2,1)}) %all-gather.26.cloned.1.call-update) | async-done | bytes 4456464 | tf_op jit(solution)/shard_map/all_gather | solution.py:93
  366.6 6.4 copy.74
  374.2 118.2 %while.28 = (s32[]{:T(128)}, bf16[17,1,512,64]{2,3,1,0:T(8,128)(2,1)}, f32[17,1,512]{2,1,0:T(1,128)S(1)}, s32[17]{0:T(128)S(1)}, bf16[1,512,1088]{2,1,0:T(8,128)...) while((s32[]{:T(128)}, ...), condition=%wide.region_5.6_spmd.clone, body=%wide.region_2.5_spmd.clone.sunk | while | flops 277872128 | bytes 13917879 | solution.py:125
  447.8 3.0 fusion.129
  492.4 4.2 fusion.91
  497.9 32.5 %multiply_convert_fusion.1 = (bf16[512,4352]{1,0:T(8,128)(2,1)}, f32[512,4352]{1,0:T(8,128)}, f32[512,4352]{1,0:T(8,128)}) fusion(f32[4352]{0:T(1024)S(1)} %reshape.501, bf16[1088,4352]{1,0:T(8,128)(2,1)} %reshape.479, f32[512,1088]{0,1:T(8,128)S(1)} %get-tuple-element.318, f32[1088]{0:T(1024)S(1)} %reshape.500, f32[1088]{0:T(1024)S(1)} %reshape.499, ...), kind=kOutput, calls=%fused_computation.72 | convolution fusion | flops 4998463488 | bytes 34010624 | tf_op jit(solution)/shard_map/dot_general | solution.py:135
  530.5 18.5 %convert_reduce_fusion = (f32[4352]{0:T(1024)}, bf16[512,4352]{1,0:T(8,128)(2,1)}) fusion(f32[512,4352]{1,0:T(8,128)} %get-tuple-element.297, bf16[4352,1088]{1,0:T(8,128)(2,1)} %all-gather.16.cloned.1.call-done, bf16[1,512,1088]{1,2,0:T(8,128)(2,1)S(1)} %copy-done.12, f32[512,4352]{1,0:T(8,128)} %get-tuple-element.319, f32[4352]{0:T(1024)S(1)} %reshape.501), kind=kOutput, calls=%fused_computation.71 | convolution fusion | flops 4886491136 | bytes 32901120 | tf_op jit(solution)/shard_map/rd,fd->rf/dot_general | solution.py:156
  549.0 10.0 multiply_reduce_fusion.1
  566.4 225.5 %while.29 = (s32[]{:T(128)}, bf16[17,1,512,64]{2,3,1,0:T(8,128)(2,1)}, bf16[17,1,2048,64]{2,3,1,0:T(8,128)(2,1)}, bf16[17,1,2048,64]{2,3,1,0:T(8,128)(2,1)}, s32...) while((s32[]{:T(128)}, ...), condition=%wide.region_12.13_spmd.clone, body=%wide.region_10.12_spmd.clone.sunk | while | flops 681737728 | bytes 34619096 | solution.py:201
  793.6 10.0 convolution_convert_fusion.1
  803.6 18.7 %reshape.494 = bf16[4,272,4,1088]{3,2,1,0:T(4,128)(2,1)} reshape(bf16[1088,4352]{1,0:T(8,128)(2,1)} %convolution_convert_fusion.1) | data formatting | bytes 18939904 | tf_op jit(solution)/shard_map/reshape | solution.py:224
  822.3 8.9 copy.84
  832.4 11.8 convolution_convert_fusion
  845.5 4.4 convolution_convert_fusion.3
  849.8 7.9 copy.81
  857.8 13.8 reduce-scatter.12.cloned.1.call-done
  871.6 83.9 %reduce-scatter.14.cloned.1.call-done = bf16[1,512,1088]{1,2,0:T(8,128)(2,1)} async-done(((bf16[1,2048,1088]{1,2,0:T(8,128)(2,1)}), bf16[1,512,1088]{1,2,0:T(8,128)(2,1)}) %reduce-scatter.14.cloned.1.call-update) | async-done | bytes 1114128 | tf_op jit(solution)/shard_map/reduce_scatter | solution.py:207
  955.5 8.3 convolution_convert_fusion.2
  963.8 19.8 %reshape.485 = bf16[4,272,3,1088]{3,2,1,0:T(4,128)(2,1)} reshape(bf16[1088,3264]{1,0:T(8,128)(2,1)} %convolution_convert_fusion.2) | data formatting | bytes 14204928 | tf_op jit(solution)/shard_map/reshape | solution.py:224
  983.5 13.9 pad_maximum_fusion
  997.4 9.0 copy.82
  1006.5 88.7 %reduce-scatter.18.cloned.1.call-done = bf16[136,1088]{1,0:T(8,128)(2,1)} async-done(((bf16[4352,1088]{1,0:T(8,128)(2,1)}), bf16[136,1088]{1,0:T(8,128)(2,1)}) %reduce-scatter.18.cloned.1.call-update) | async-done | bytes 295952
  1095.3 138.1 %reduce-scatter.20.cloned.1.call-done = bf16[136,1088]{1,0:T(8,128)(2,1)} async-done(((bf16[4352,1088]{1,0:T(8,128)(2,1)}), bf16[136,1088]{1,0:T(8,128)(2,1)}) %reduce-scatter.20.cloned.1.call-update) | async-done | bytes 295952
  1233.7 137.7 %reduce-scatter.16.cloned.1.call-done = bf16[136,1088]{1,0:T(8,128)(2,1)} async-done(((bf16[4352,1088]{1,0:T(8,128)(2,1)}), bf16[136,1088]{1,0:T(8,128)(2,1)}) %reduce-scatter.16.cloned.1.call-update) | async-done | bytes 295952
  1371.4 13.9 fusion.57
  1388.1 8.2 fusion.83
  1401.1 40.4 %psum.7 = f32[4,3264]{1,0:T(4,128)S(1)} all-reduce(f32[4,3264]{1,0:T(4,128)S(1)} %concatenate.34), channel_id=1, replica_groups=mesh['rep'=8,'fsdp'=4] {'rep','fsdp'}, use_global_device_ids=true, to_apply=%region_26.27 | all-reduce | flops 13056 | bytes 104448 | tf_op jit(solution)/shard_map/psum | solution.py:253
  1445.5 4.2 copy.85
  1449.7 6.5 reshape.504
  1456.3 4.3 convert_element_type.291
  1460.6 4.0 all-gather.18.cloned.1.call-done
  1466.1 3.2 copy.93
  1469.3 6.7 reshape.503
  (426 shorter events, 364.6 us)
Async XLA Ops:
  7.2 146.7 %copy-start = (bf16[1088,1088]{1,0:T(8,128)(2,1)S(1)}, bf16[1088,1088]{1,0:T(8,128)(2,1)}, u32[]{:S(2)}) copy-start(bf16[1088,1088]{1,0:T(8,128)(2,1)} %param.25) | copy-start | bytes 7102468
  7.2 6.0 copy-start.20
  7.2 102.0 %all-gather.12.cloned.1.call-start = ((), (), s32[]{:S(2)}) async-start(), calls=%async_computation.5 | async-start | bytes 10340352 | tf_op jit(solution)/shard_map/all_gather | solution.py:51
  22.0 173.3 %all-gather.14.cloned.1.call-start = ((), (), s32[]{:S(2)}) async-start(), calls=%async_computation.6 | async-start | bytes 10340352 | tf_op jit(solution)/shard_map/all_gather | solution.py:51
  28.4 4.2 copy-start.35
  28.4 4.2 copy-start.36
  28.4 4.2 copy-start.37
  28.4 4.3 copy-start.38
  28.4 4.2 copy-start.39
  28.4 4.2 copy-start.40
  28.4 4.2 copy-start.41
  28.4 4.2 copy-start.42
  31.3 249.8 %all-gather.24.cloned.1.call-start = ((), (), s32[]{:S(2)}) async-start(), calls=%async_computation.13 | async-start | bytes 5570560 | tf_op jit(solution)/shard_map/all_gather | solution.py:92
  55.0 88.0 %copy-start.21 = (f32[1088]{0:T(1024)}, f32[1088]{0:T(1024)S(1)}, u32[]{:S(2)}) copy-start(f32[1088]{0:T(1024)S(1)} %reshape.496) | copy-start | bytes 13060
  55.3 87.7 %copy-start.33 = (f32[1088]{0:T(1024)}, f32[1088]{0:T(1024)S(1)}, u32[]{:S(2)}) copy-start(f32[1088]{0:T(1024)S(1)} %reshape.497) | copy-start | bytes 13060
  56.9 86.2 %copy-start.23 = (f32[512]{0:T(512)}, f32[512]{0:T(512)S(1)}, u32[]{:S(2)}) copy-start(f32[512]{0:T(512)S(1)} %broadcast_multiply_fusion.1) | copy-start | bytes 6148
  58.5 54.4 %copy-start.27 = (f32[512]{0:T(512)}, f32[512]{0:T(512)S(1)}, u32[]{:S(2)}) copy-start(f32[512]{0:T(512)S(1)} %fusion.64) | copy-start | bytes 6148
  58.5 84.5 %copy-start.29 = (f32[512]{0:T(512)}, f32[512]{0:T(512)S(1)}, u32[]{:S(2)}) copy-start(f32[512]{0:T(512)S(1)} %fusion.77) | copy-start | bytes 6148
  153.2 213.4 %all-gather.26.cloned.1.call-start = ((), (), s32[]{:S(2)}) async-start(), calls=%async_computation.14 | async-start | bytes 5570560 | tf_op jit(solution)/shard_map/all_gather | solution.py:93
  153.8 376.6 %all-gather.16.cloned.1.call-start = ((), (), s32[]{:S(2)}) async-start(), calls=%async_computation.7 | async-start | bytes 10340352 | tf_op jit(solution)/shard_map/all_gather | solution.py:51
  154.6 4.1 copy-start.11
  154.6 717.0 %reduce-scatter.12.cloned.1.call-start = ((), (), s32[]{:S(2)}) async-start(), calls=%async_computation.8 | async-start | bytes 5570560 | tf_op jit(solution)/shard_map/reduce_scatter | solution.py:206
  374.2 118.2 %copy-start.4 = (bf16[1,512,1088]{1,2,0:T(8,128)(2,1)S(1)}, bf16[1,512,1088]{1,2,0:T(8,128)(2,1)}, u32[]{:S(2)}) copy-start(bf16[1,512,1088]{1,2,0:T(8,128)(2,1)} %param.18) | copy-start | bytes 3342340
  492.4 4.2 copy-start.10
  497.9 32.5 %copy-start.12 = (bf16[1,512,1088]{1,2,0:T(8,128)(2,1)S(1)}, bf16[1,512,1088]{1,2,0:T(8,128)(2,1)}, u32[]{:S(2)}) copy-start(bf16[1,512,1088]{1,2,0:T(8,128)(2,1)} %param.31) | copy-start | bytes 3342340
  530.4 18.5 %copy-start.8 = (f32[512,1088]{0,1:T(8,128)S(1)}, f32[512,1088]{0,1:T(8,128)}, u32[]{:S(2)}) copy-start(f32[512,1088]{0,1:T(8,128)} %copy-done.7) | copy-start | bytes 6684676
  559.7 5.6 copy-start.2
  559.7 3.0 copy-start.16
  559.7 5.6 copy-start.31
  560.7 4.6 copy-start.18
  792.0 163.5 %reduce-scatter.14.cloned.1.call-start = ((), (), s32[]{:S(2)}) async-start(), calls=%async_computation.9 | async-start | bytes 5570560 | tf_op jit(solution)/shard_map/reduce_scatter | solution.py:207
  792.7 302.5 %reduce-scatter.18.cloned.1.call-start = ((), (), s32[]{:S(2)}) async-start(), calls=%async_computation.16 | async-start | bytes 10340352
  831.2 402.2 %reduce-scatter.20.cloned.1.call-start = ((), (), s32[]{:S(2)}) async-start(), calls=%async_computation.17 | async-start | bytes 10340352
  844.2 527.1 %reduce-scatter.16.cloned.1.call-start = ((), (), s32[]{:S(2)}) async-start(), calls=%async_computation.15 | async-start | bytes 10340352
  849.8 105.6 %copy-start.5 = (bf16[1,512,1088]{1,2,0:T(8,128)(2,1)S(1)}, bf16[1,512,1088]{1,2,0:T(8,128)(2,1)}, u32[]{:S(2)}) copy-start(bf16[1,512,1088]{1,2,0:T(8,128)(2,1)} %param.18) | copy-start | bytes 3342340
  849.8 105.6 %copy-start.22 = (f32[1088]{0:T(1024)S(1)}, f32[1088]{0:T(1024)}, u32[]{:S(2)}) copy-start(f32[1088]{0:T(1024)} %copy-done.21) | copy-start | bytes 13060
  849.8 105.6 %copy-start.24 = (f32[512]{0:T(512)S(1)}, f32[512]{0:T(512)}, u32[]{:S(2)}) copy-start(f32[512]{0:T(512)} %copy-done.23) | copy-start | bytes 6148
  849.8 105.6 %copy-start.30 = (f32[512]{0:T(512)S(1)}, f32[512]{0:T(512)}, u32[]{:S(2)}) copy-start(f32[512]{0:T(512)} %copy-done.29) | copy-start | bytes 6148
  849.8 105.6 %copy-start.34 = (f32[1088]{0:T(1024)S(1)}, f32[1088]{0:T(1024)}, u32[]{:S(2)}) copy-start(f32[1088]{0:T(1024)} %copy-done.33) | copy-start | bytes 13060
  1006.4 227.2 %copy-start.25 = (f32[4,272]{1,0:T(4,128)S(1)}, f32[4,272]{1,0:T(4,128)}, u32[]{:S(2)}) copy-start(f32[4,272]{1,0:T(4,128)} %get-tuple-element.307) | copy-start | bytes 13060
  1006.5 437.0 %all-gather.20.cloned.1.call-start = ((), (), s32[]{:S(2)}) async-start(), calls=%async_computation.11 | async-start | bytes 2820096 | tf_op jit(solution)/shard_map/all_gather | solution.py:229
  1095.2 361.0 %all-gather.22.cloned.1.call-start = ((), (), s32[]{:S(2)}) async-start(), calls=%async_computation.12 | async-start | bytes 2820096 | tf_op jit(solution)/shard_map/all_gather | solution.py:229
  1233.4 231.2 %all-gather.18.cloned.1.call-start = ((), (), s32[]{:S(2)}) async-start(), calls=%async_computation.10 | async-start | bytes 2820096 | tf_op jit(solution)/shard_map/all_gather | solution.py:229
  1371.4 14.1 copy-start.26
  1371.4 14.2 copy-start.17
  1388.1 8.3 copy-start.28
  1388.1 8.3 copy-start.6
  1469.3 8.9 copy-start.1
  (10 other events, 16.7 us)
Sparse Core Ops, SparseCore 0:
  22.1 87.0 all-gather.11
  112.7 82.5 all-gather.13
  197.5 83.5 all-gather.23
  283.1 83.4 all-gather.25
  369.4 82.4 all-gather.15
  792.1 79.4 reduce-scatter.11
  873.9 81.5 reduce-scatter.13
  961.6 133.5 reduce-scatter.17
  1101.3 132.0 reduce-scatter.19
  1239.3 131.9 reduce-scatter.15
  1373.3 28.4 all-gather.19
  1403.5 29.6 all-gather.21
  1435.1 29.4 all-gather.17
where the time goes:
time: 1500 us; the launch traced here: 1480 us
  waiting for transfers between devices  693 us (46%)
  matrix products  414 us (28%)
  local copies, waits for them, and re-layouts  220 us (15%)
  blocking collectives  61.5 us (4%)
  other arithmetic  57.4 us (4%)
  loops' own time  23 us (2%)
  between operations  15.4 us (1%)
    unnamed x16, waiting for transfers between devices  366 us
    all_gather x3, waiting for transfers between devices, gather_all(): return lax.all_gather(own_piece(matrix), everyone, axis=0, tiled=True)  86.7 us
    reduce_scatter x1, waiting for transfers between devices, local(): lax.psum_scatter(value_grads.astype(jnp.bfloat16), 'fsdp', scatter_dimens...  83.9 us
    dot_general x34, matrix products, head_scores(): jnp.einsum('sqd,skd->sqk', query_part, key_part, preferred_element_type=j...  83.4 us
    all_gather x1, waiting for transfers between devices, local(): lax.all_gather(values, 'fsdp', axis=1, tiled=True)  79.1 us
    all_gather x1, waiting for transfers between devices, local(): lax.all_gather(keys, 'fsdp', axis=1, tiled=True)  59.5 us
    dot_general x17, matrix products, head_forward(): jnp.einsum('sqk,skd->sqd', probabilities, value_part, preferred_element_t...  48.9 us
    reshape x3, local copies, waits for them, and re-layouts, grad_units(): matrix.astype(jnp.bfloat16).reshape(fsdp, rows, blocks, features)  47.3 us
  transfers between devices with their start and end apart: 13, of which 10 were waited for; matrix products, arithmetic and copies ran while one was open for 27% of the time, Pallas kernels for 0%

commit v1 on v0

--- a/solution.py
+++ b/solution.py
@@ -250,7 +250,8 @@
         grad_shift_two,
     )
     stacked = jnp.concatenate([g.reshape(fsdp, -1) for g in small_grads], 1)
-    stacked = lax.psum(stacked, ("rep", "fsdp"))
+    review_islands = lambda t0: jnp.sum(lax.all_gather(t0, ("rep", "fsdp")), 0)
+    stacked = review_islands(stacked)
     mine = lax.dynamic_index_in_dim(stacked, lax.axis_index("fsdp"), 0, keepdims=False)
     small_own = []
     start = 0

time: 1500 us -> 1550 us (1.033)
  waiting for transfers between devices: 693 us -> 787 us
  blocking collectives: 61.5 us -> 21.1 us
    all_gather x3, waiting for transfers between devices: 4.04 us -> 72 us  [reduce_all(): return lax.all_gather(part, 'rep', axis=0, tiled=True)]
    all_gather x0 -> x1, waiting for transfers between devices: none -> 43.7 us  [local(): review_islands = lambda t0: jnp.sum(lax.all_gather(t0, ('rep', 'fsdp')), 0)]
    psum x1 -> x0, blocking collectives: 40.4 us -> none  [local(): stacked = lax.psum(stacked, ('rep', 'fsdp'))]
    unnamed x16 -> x17, waiting for transfers between devices: 366 us -> 349 us
    unnamed x95 -> x89, local copies, waits for them, and re-layouts: 32.7 us -> 33.3 us
  transfers between devices with their start and end apart: 13 -> 14, of which waited for: 10 -> 13; matrix products, arithmetic and copies ran while one was open for 27% -> 27% of each run, Pallas kernels for 0% -> 0%
where the time goes in v1:
time: 1550 us; the launch traced here: 1540 us
  waiting for transfers between devices  787 us (51%)
  matrix products  412 us (27%)
  local copies, waits for them, and re-layouts  221 us (14%)
  other arithmetic  59.4 us (4%)
  loops' own time  23 us (1%)
  blocking collectives  21.1 us (1%)
    unnamed x17, waiting for transfers between devices  349 us
    all_gather x3, waiting for transfers between devices, gather_all(): return lax.all_gather(own_piece(matrix), everyone, axis=0, tiled=True)  86.6 us
    reduce_scatter x1, waiting for transfers between devices, local(): lax.psum_scatter(value_grads.astype(jnp.bfloat16), 'fsdp', scatter_dimens...  83.9 us
    dot_general x34, matrix products, head_scores(): jnp.einsum('sqd,skd->sqk', query_part, key_part, preferred_element_type=j...  83.4 us
    all_gather x1, waiting for transfers between devices, local(): lax.all_gather(values, 'fsdp', axis=1, tiled=True)  79.1 us
    all_gather x3, waiting for transfers between devices, reduce_all(): return lax.all_gather(part, 'rep', axis=0, tiled=True)  72 us
    all_gather x1, waiting for transfers between devices, local(): lax.all_gather(keys, 'fsdp', axis=1, tiled=True)  59.5 us
    dot_general x17, matrix products, head_forward(): jnp.einsum('sqk,skd->sqd', probabilities, value_part, preferred_element_t...  48.7 us
  transfers between devices with their start and end apart: 14, of which 13 were waited for; matrix products, arithmetic and copies ran while one was open for 27% of the time, Pallas kernels for 0%

profile of v1, /device:TPU:0, one launch (start us, length us, event | category | flops | bytes accessed | tf_op | source)
XLA Modules:
  0.0 1541.3 jit_solution(3148637956026607438)
XLA Ops:
  7.3 5.9 reshape.469
  14.2 4.4 pad_maximum_fusion.1
  22.1 6.3 reshape.476
  33.1 21.1 %all-reduce = bf16[13056]{0:T(1024)(128)(2,1)S(1)} all-reduce(bf16[13056]{0:T(1024)(128)(2,1)S(1)} %dynamic-update-slice), channel_id=2, replica_groups=mesh['rep'=8,'fsdp'=4] {'fsdp'}, use_global_device_ids=true, to_apply=%add | all-reduce | flops 13056 | bytes 52224
  58.5 50.7 %all-gather.15.cloned.1.call-done = bf16[4352,1088]{1,0:T(8,128)(2,1)} async-done(((bf16[136,1088]{1,0:T(8,128)(2,1)}), bf16[4352,1088]{1,0:T(8,128)(2,1)}) %all-gather.15.cloned.1.call-update) | async-done | bytes 9469968 | tf_op jit(solution)/shard_map/all_gather | solution.py:51
  109.2 3.7 slice.164
  112.9 10.9 copy.91
  123.8 19.2 %reshape.472 = bf16[1088,3264]{1,0:T(8,128)(2,1)} reshape(bf16[4,272,3,1088]{3,2,1,0:T(4,128)(2,1)} %bitcast.242) | data formatting | bytes 14204928 | tf_op jit(solution)/shard_map/reshape | solution.py:55
  143.0 8.3 add_convert_fusion
  155.3 3.4 slice.171
  159.4 35.9 %all-gather.17.cloned.1.call-done = bf16[4352,1088]{1,0:T(8,128)(2,1)} async-done(((bf16[136,1088]{1,0:T(8,128)(2,1)}), bf16[4352,1088]{1,0:T(8,128)(2,1)}) %all-gather.17.cloned.1.call-update) | async-done | bytes 9469968 | tf_op jit(solution)/shard_map/all_gather | solution.py:51
  195.3 9.7 copy.92
  205.0 16.7 %reshape.479 = bf16[1088,4352]{1,0:T(8,128)(2,1)} reshape(bf16[4,272,4,1088]{3,2,1,0:T(4,128)(2,1)} %bitcast.241) | data formatting | bytes 18939904 | tf_op jit(solution)/shard_map/reshape | solution.py:55
  221.6 59.5 %all-gather.27.cloned.1.call-done = bf16[2048,1088]{0,1:T(8,128)(2,1)} async-done(((bf16[512,1088]{0,1:T(8,128)(2,1)}), bf16[2048,1088]{0,1:T(8,128)(2,1)}) %all-gather.27.cloned.1.call-update) | async-done | bytes 4456464 | tf_op jit(solution)/shard_map/all_gather | solution.py:92
  281.1 6.4 copy.73
  287.5 79.1 %all-gather.29.cloned.1.call-done = bf16[2048,1088]{0,1:T(8,128)(2,1)} async-done(((bf16[512,1088]{0,1:T(8,128)(2,1)}), bf16[2048,1088]{0,1:T(8,128)(2,1)}) %all-gather.29.cloned.1.call-update) | async-done | bytes 4456464 | tf_op jit(solution)/shard_map/all_gather | solution.py:93
  366.6 6.4 copy.74
  374.2 118.0 %while.28 = (s32[]{:T(128)}, bf16[17,1,512,64]{2,3,1,0:T(8,128)(2,1)}, f32[17,1,512]{2,1,0:T(1,128)S(1)}, s32[17]{0:T(128)S(1)}, bf16[1,512,1088]{2,1,0:T(8,128)...) while((s32[]{:T(128)}, ...), condition=%wide.region_5.6_spmd.clone, body=%wide.region_2.5_spmd.clone.sunk | while | flops 277872128 | bytes 13917879 | solution.py:125
  492.2 4.2 fusion.91
  497.8 32.4 %multiply_convert_fusion.1 = (bf16[512,4352]{1,0:T(8,128)(2,1)}, f32[512,4352]{1,0:T(8,128)}, f32[512,4352]{1,0:T(8,128)}) fusion(f32[4352]{0:T(1024)S(1)} %reshape.501, bf16[1088,4352]{1,0:T(8,128)(2,1)} %reshape.479, f32[512,1088]{0,1:T(8,128)S(1)} %get-tuple-element.318, f32[1088]{0:T(1024)S(1)} %reshape.500, f32[1088]{0:T(1024)S(1)} %reshape.499, ...), kind=kOutput, calls=%fused_computation.72 | convolution fusion | flops 4998463488 | bytes 34010624 | tf_op jit(solution)/shard_map/dot_general | solution.py:135
  530.3 18.0 %convert_reduce_fusion = (f32[4352]{0:T(1024)S(1)}, bf16[512,4352]{1,0:T(8,128)(2,1)}) fusion(f32[512,4352]{1,0:T(8,128)} %get-tuple-element.297, bf16[4352,1088]{1,0:T(8,128)(2,1)} %all-gather.19.cloned.1.call-done, bf16[1,512,1088]{1,2,0:T(8,128)(2,1)S(1)} %copy-done.12, f32[512,4352]{1,0:T(8,128)} %get-tuple-element.319, f32[4352]{0:T(1024)S(1)} %reshape.501), kind=kOutput, calls=%fused_computation.71 | convolution fusion | flops 4886491136 | bytes 32901120 | tf_op jit(solution)/shard_map/rd,fd->rf/dot_general | solution.py:156
  548.2 10.0 multiply_reduce_fusion.1
  565.7 225.4 %while.29 = (s32[]{:T(128)}, bf16[17,1,512,64]{2,3,1,0:T(8,128)(2,1)}, bf16[17,1,2048,64]{2,3,1,0:T(8,128)(2,1)}, bf16[17,1,2048,64]{2,3,1,0:T(8,128)(2,1)}, s32...) while((s32[]{:T(128)}, ...), condition=%wide.region_12.13_spmd.clone, body=%wide.region_10.12_spmd.clone.sunk | while | flops 681737728 | bytes 34619096 | solution.py:201
  792.8 10.0 convolution_convert_fusion.1
  802.8 18.7 %reshape.494 = bf16[4,272,4,1088]{3,2,1,0:T(4,128)(2,1)} reshape(bf16[1088,4352]{1,0:T(8,128)(2,1)} %convolution_convert_fusion.1) | data formatting | bytes 18939904 | tf_op jit(solution)/shard_map/reshape | solution.py:224
  821.5 8.9 copy.84
  831.6 11.8 convolution_convert_fusion
  844.6 4.4 convolution_convert_fusion.3
  849.0 7.9 copy.81
  857.0 13.8 reduce-scatter.12.cloned.1.call-done
  870.8 83.9 %reduce-scatter.14.cloned.1.call-done = bf16[1,512,1088]{1,2,0:T(8,128)(2,1)} async-done(((bf16[1,2048,1088]{1,2,0:T(8,128)(2,1)}), bf16[1,512,1088]{1,2,0:T(8,128)(2,1)}) %reduce-scatter.14.cloned.1.call-update) | async-done | bytes 1114128 | tf_op jit(solution)/shard_map/reduce_scatter | solution.py:207
  954.7 8.3 convolution_convert_fusion.2
  963.0 19.8 %reshape.485 = bf16[4,272,3,1088]{3,2,1,0:T(4,128)(2,1)} reshape(bf16[1088,3264]{1,0:T(8,128)(2,1)} %convolution_convert_fusion.2) | data formatting | bytes 14204928 | tf_op jit(solution)/shard_map/reshape | solution.py:224
  982.8 13.9 pad_maximum_fusion
  996.7 9.0 copy.82
  1009.7 8.0 fusion.83
  1023.1 71.4 %reduce-scatter.18.cloned.1.call-done = bf16[136,1088]{1,0:T(8,128)(2,1)} async-done(((bf16[4352,1088]{1,0:T(8,128)(2,1)}), bf16[136,1088]{1,0:T(8,128)(2,1)}) %reduce-scatter.18.cloned.1.call-update) | async-done | bytes 295952
  1094.6 138.1 %reduce-scatter.20.cloned.1.call-done = bf16[136,1088]{1,0:T(8,128)(2,1)} async-done(((bf16[4352,1088]{1,0:T(8,128)(2,1)}), bf16[136,1088]{1,0:T(8,128)(2,1)}) %reduce-scatter.20.cloned.1.call-update) | async-done | bytes 295952
  1232.8 137.8 %reduce-scatter.16.cloned.1.call-done = bf16[136,1088]{1,0:T(8,128)(2,1)} async-done(((bf16[4352,1088]{1,0:T(8,128)(2,1)}), bf16[136,1088]{1,0:T(8,128)(2,1)}) %reduce-scatter.16.cloned.1.call-update) | async-done | bytes 295952
  1370.7 13.8 fusion.57
  1384.5 43.7 %all-gather.31.cloned.1.call-done = f32[32,4,3264]{2,1,0:T(4,128)} async-done(((f32[1,4,3264]{2,1,0:T(4,128)}), f32[32,4,3264]{2,1,0:T(4,128)}) %all-gather.31.cloned.1.call-update) | async-done | bytes 1671184 | tf_op jit(solution)/shard_map/all_gather | solution.py:253
  1431.8 26.5 %all-gather.23.cloned.1.call-done = bf16[1088,1088]{1,0:T(8,128)(2,1)} async-done(((bf16[136,1088]{1,0:T(8,128)(2,1)}), bf16[1088,1088]{1,0:T(8,128)(2,1)}) %all-gather.23.cloned.1.call-update) | async-done | bytes 2367504 | tf_op jit(solution)/shard_map/all_gather | solution.py:229
  1460.4 4.2 copy.85
  1464.6 6.6 reshape.504
  1471.2 18.5 %all-gather.25.cloned.1.call-done = bf16[1088,1088]{1,0:T(8,128)(2,1)} async-done(((bf16[136,1088]{1,0:T(8,128)(2,1)}), bf16[1088,1088]{1,0:T(8,128)(2,1)}) %all-gather.25.cloned.1.call-update) | async-done | bytes 2367504 | tf_op jit(solution)/shard_map/all_gather | solution.py:229
  1489.8 4.3 convert_element_type.291
  1494.1 26.9 %all-gather.21.cloned.1.call-done = bf16[1088,1088]{1,0:T(8,128)(2,1)} async-done(((bf16[136,1088]{1,0:T(8,128)(2,1)}), bf16[1088,1088]{1,0:T(8,128)(2,1)}) %all-gather.21.cloned.1.call-update) | async-done | bytes 2367504 | tf_op jit(solution)/shard_map/all_gather | solution.py:229
  1525.7 6.7 reshape.503
  (423 shorter events, 373.9 us)
Async XLA Ops:
  7.2 146.6 %copy-start = (bf16[1088,1088]{1,0:T(8,128)(2,1)S(1)}, bf16[1088,1088]{1,0:T(8,128)(2,1)}, u32[]{:S(2)}) copy-start(bf16[1088,1088]{1,0:T(8,128)(2,1)} %param.25) | copy-start | bytes 7102468
  7.2 6.0 copy-start.20
  7.2 102.0 %all-gather.15.cloned.1.call-start = ((), (), s32[]{:S(2)}) async-start(), calls=%async_computation.5 | async-start | bytes 10340352 | tf_op jit(solution)/shard_map/all_gather | solution.py:51
  22.0 173.3 %all-gather.17.cloned.1.call-start = ((), (), s32[]{:S(2)}) async-start(), calls=%async_computation.6 | async-start | bytes 10340352 | tf_op jit(solution)/shard_map/all_gather | solution.py:51
  28.3 3.0 copy-start.40
  28.4 4.2 copy-start.32
  28.4 4.2 copy-start.33
  28.4 4.2 copy-start.34
  28.4 4.3 copy-start.35
  28.4 4.2 copy-start.36
  28.4 4.2 copy-start.37
  28.4 4.2 copy-start.38
  28.4 4.2 copy-start.39
  31.3 249.8 %all-gather.27.cloned.1.call-start = ((), (), s32[]{:S(2)}) async-start(), calls=%async_computation.13 | async-start | bytes 5570560 | tf_op jit(solution)/shard_map/all_gather | solution.py:92
  55.0 88.0 %copy-start.21 = (f32[1088]{0:T(1024)}, f32[1088]{0:T(1024)S(1)}, u32[]{:S(2)}) copy-start(f32[1088]{0:T(1024)S(1)} %reshape.496) | copy-start | bytes 13060
  55.3 87.7 %copy-start.30 = (f32[1088]{0:T(1024)}, f32[1088]{0:T(1024)S(1)}, u32[]{:S(2)}) copy-start(f32[1088]{0:T(1024)S(1)} %reshape.497) | copy-start | bytes 13060
  56.9 86.1 %copy-start.23 = (f32[512]{0:T(512)}, f32[512]{0:T(512)S(1)}, u32[]{:S(2)}) copy-start(f32[512]{0:T(512)S(1)} %broadcast_multiply_fusion.1) | copy-start | bytes 6148
  58.5 54.4 %copy-start.26 = (f32[512]{0:T(512)}, f32[512]{0:T(512)S(1)}, u32[]{:S(2)}) copy-start(f32[512]{0:T(512)S(1)} %fusion.64) | copy-start | bytes 6148
  58.5 84.5 %copy-start.28 = (f32[512]{0:T(512)}, f32[512]{0:T(512)S(1)}, u32[]{:S(2)}) copy-start(f32[512]{0:T(512)S(1)} %fusion.77) | copy-start | bytes 6148
  153.2 213.4 %all-gather.29.cloned.1.call-start = ((), (), s32[]{:S(2)}) async-start(), calls=%async_computation.14 | async-start | bytes 5570560 | tf_op jit(solution)/shard_map/all_gather | solution.py:93
  153.8 376.5 %all-gather.19.cloned.1.call-start = ((), (), s32[]{:S(2)}) async-start(), calls=%async_computation.7 | async-start | bytes 10340352 | tf_op jit(solution)/shard_map/all_gather | solution.py:51
  154.6 4.1 copy-start.11
  154.6 716.2 %reduce-scatter.12.cloned.1.call-start = ((), (), s32[]{:S(2)}) async-start(), calls=%async_computation.8 | async-start | bytes 5570560 | tf_op jit(solution)/shard_map/reduce_scatter | solution.py:206
  374.2 118.0 %copy-start.4 = (bf16[1,512,1088]{1,2,0:T(8,128)(2,1)S(1)}, bf16[1,512,1088]{1,2,0:T(8,128)(2,1)}, u32[]{:S(2)}) copy-start(bf16[1,512,1088]{1,2,0:T(8,128)(2,1)} %param.18) | copy-start | bytes 3342340
  492.2 4.2 copy-start.10
  497.8 32.5 %copy-start.12 = (bf16[1,512,1088]{1,2,0:T(8,128)(2,1)S(1)}, bf16[1,512,1088]{1,2,0:T(8,128)(2,1)}, u32[]{:S(2)}) copy-start(bf16[1,512,1088]{1,2,0:T(8,128)(2,1)} %param.31) | copy-start | bytes 3342340
  530.3 18.0 %copy-start.8 = (f32[512,1088]{0,1:T(8,128)S(1)}, f32[512,1088]{0,1:T(8,128)}, u32[]{:S(2)}) copy-start(f32[512,1088]{0,1:T(8,128)} %copy-done.7) | copy-start | bytes 6684676
  558.9 5.6 copy-start.2
  558.9 3.0 copy-start.16
  560.0 4.6 copy-start.17
  791.1 163.5 %reduce-scatter.14.cloned.1.call-start = ((), (), s32[]{:S(2)}) async-start(), calls=%async_computation.9 | async-start | bytes 5570560 | tf_op jit(solution)/shard_map/reduce_scatter | solution.py:207
  791.9 302.6 %reduce-scatter.18.cloned.1.call-start = ((), (), s32[]{:S(2)}) async-start(), calls=%async_computation.17 | async-start | bytes 10340352
  830.4 402.3 %reduce-scatter.20.cloned.1.call-start = ((), (), s32[]{:S(2)}) async-start(), calls=%async_computation.18 | async-start | bytes 10340352
  843.4 527.1 %reduce-scatter.16.cloned.1.call-start = ((), (), s32[]{:S(2)}) async-start(), calls=%async_computation.16 | async-start | bytes 10340352
  849.0 105.7 %copy-start.5 = (bf16[1,512,1088]{1,2,0:T(8,128)(2,1)S(1)}, bf16[1,512,1088]{1,2,0:T(8,128)(2,1)}, u32[]{:S(2)}) copy-start(bf16[1,512,1088]{1,2,0:T(8,128)(2,1)} %param.18) | copy-start | bytes 3342340
  849.0 105.7 %copy-start.22 = (f32[1088]{0:T(1024)S(1)}, f32[1088]{0:T(1024)}, u32[]{:S(2)}) copy-start(f32[1088]{0:T(1024)} %copy-done.21) | copy-start | bytes 13060
  849.0 105.7 %copy-start.24 = (f32[512]{0:T(512)S(1)}, f32[512]{0:T(512)}, u32[]{:S(2)}) copy-start(f32[512]{0:T(512)} %copy-done.23) | copy-start | bytes 6148
  849.0 105.7 %copy-start.29 = (f32[512]{0:T(512)S(1)}, f32[512]{0:T(512)}, u32[]{:S(2)}) copy-start(f32[512]{0:T(512)} %copy-done.28) | copy-start | bytes 6148
  849.0 105.7 %copy-start.31 = (f32[1088]{0:T(1024)S(1)}, f32[1088]{0:T(1024)}, u32[]{:S(2)}) copy-start(f32[1088]{0:T(1024)} %copy-done.30) | copy-start | bytes 13060
  1005.7 422.5 %all-gather.31.cloned.1.call-start = ((), (), s32[]{:S(2)}) async-start(), calls=%async_computation.15 | async-start | bytes 1757184 | tf_op jit(solution)/shard_map/all_gather | solution.py:253
  1009.7 8.0 copy-start.27
  1009.7 8.0 copy-start.6
  1017.6 2.0 copy-start.15
  1019.6 351.0 %copy-start.25 = (f32[4,272]{1,0:T(4,128)S(1)}, f32[4,272]{1,0:T(4,128)}, u32[]{:S(2)}) copy-start(f32[4,272]{1,0:T(4,128)} %get-tuple-element.307) | copy-start | bytes 13060
  1023.1 435.3 %all-gather.23.cloned.1.call-start = ((), (), s32[]{:S(2)}) async-start(), calls=%async_computation.11 | async-start | bytes 2820096 | tf_op jit(solution)/shard_map/all_gather | solution.py:229
  1094.5 395.2 %all-gather.25.cloned.1.call-start = ((), (), s32[]{:S(2)}) async-start(), calls=%async_computation.12 | async-start | bytes 2820096 | tf_op jit(solution)/shard_map/all_gather | solution.py:229
  1232.7 288.3 %all-gather.21.cloned.1.call-start = ((), (), s32[]{:S(2)}) async-start(), calls=%async_computation.10 | async-start | bytes 2820096 | tf_op jit(solution)/shard_map/all_gather | solution.py:229
  1525.7 8.9 copy-start.1
  (8 other events, 11.2 us)
Sparse Core Ops, SparseCore 0:
  22.1 86.9 all-gather.14
  112.7 82.5 all-gather.16
  197.4 83.5 all-gather.26
  283.1 83.4 all-gather.28
  369.4 82.4 all-gather.18
  791.3 79.4 reduce-scatter.11
  873.1 81.5 reduce-scatter.13
  960.8 133.7 reduce-scatter.17
  1100.6 132.0 reduce-scatter.19
  1238.7 131.8 reduce-scatter.15
  1374.0 54.0 all-gather.30
  1429.9 28.4 all-gather.22
  1460.2 29.4 all-gather.24
  1491.5 29.4 all-gather.20
